TPU v7x, 128 devices: a whole 4x4x4 slice. The times are simulated.
128 devices in a mesh: rx: 8 (over x, core), ry: 16 (over y, z).
Axes of the slice: x: 4, y: 4, z: 4, core: 2. Of those that a mesh axis runs over, the one named last changes fastest.
Arguments:
- column_features: bfloat16 [16384, 1536], P(('rx', 'ry')), may hold values from -6 to 6
- column_route: int32 [16384], P(('rx', 'ry')), may hold values from 0 to 32767, as said below
- cotangent: bfloat16 [128, 256, 1536], P('rx', 'ry'), may hold values from -6 to 6
- first_weight: bfloat16 [27, 96, 96], replicated, may hold values from -0.125 to 0.125
- second_weight: bfloat16 [27, 96, 96], replicated, may hold values from -0.125 to 0.125
Outputs:
- block_output: bfloat16 [128, 256, 1536], P('rx', 'ry')
- feature_grads: bfloat16 [16384, 1536], P(('rx', 'ry'))
- first_grad: float32 [27, 96, 96], replicated
- second_grad: float32 [27, 96, 96], replicated
Inputs may be any that keep to these rules, and one draw needn't show every extreme that they name: `column_route`: entries are distinct; entry o * 256 + q names slot q of owner o, owner o = i * 16 + j being the device at rx index i and ry index j. The columns of one owner are spread over the devices' shards as evenly as possible: each shard holds the floor or the ceiling of that owner's count / 128. An owner holds at most 256 columns, and in every draw one owner holds exactly 256, so that it receives 2 from every shard.
All inputs are finite; a program needn't handle non-finite values.
Results may differ from a plain program's by a relative error of at most 0.0029.
Values may be sent and summed in bfloat16 or wider, within the bound.
A program may use at most 256 MiB of HBM per device.

v0:
```python
import jax
import jax.numpy as jnp
from jax import lax
from jax.sharding import PartitionSpec as P


def extended(block, sides, width):
    for axis, dim in sides:
        count = lax.axis_size(axis)
        forward = [(i, i + 1) for i in range(count - 1)]
        backward = [(target, source) for source, target in forward]
        low = lax.ppermute(
            lax.slice_in_dim(block, block.shape[dim] - width, None, axis=dim), axis, forward
        )
        high = lax.ppermute(lax.slice_in_dim(block, 0, width, axis=dim), axis, backward)
        block = jnp.concatenate([low, block, high], axis=dim)
    return block


def pad_depth(widened, channels):
    shaped = widened.reshape(
        widened.shape[0], widened.shape[1], widened.shape[2] // channels, channels
    )
    return jnp.pad(shaped, ((0, 0), (0, 0), (1, 1), (0, 0)))


def face_field(rows, channels):
    widened = extended(rows, (("rx", 0), ("ry", 1)), 1)
    return pad_depth(widened, channels)


def conv_sum(padded, weights):
    size_x = padded.shape[0] - 2
    size_y = padded.shape[1] - 2
    size_z = padded.shape[2] - 2
    result = jnp.zeros((size_x, size_y, size_z, weights.shape[1]), jnp.float32)
    for a in range(3):
        for b in range(3):
            for c in range(3):
                piece = padded[a : a + size_x, b : b + size_y, c : c + size_z, :]
                result = result + jnp.einsum(
                    "xyzi,oi->xyzo",
                    piece,
                    weights[9 * a + 3 * b + c],
                    preferred_element_type=jnp.float32,
                )
    return result


def correlate(grads, padded):
    size_x, size_y, size_z, _ = grads.shape
    terms = []
    for a in range(3):
        for b in range(3):
            for c in range(3):
                piece = padded[a : a + size_x, b : b + size_y, c : c + size_z, :]
                terms.append(
                    jnp.einsum("xyzo,xyzi->oi", grads, piece, preferred_element_type=jnp.float32)
                )
    return jnp.stack(terms, axis=0)


def flipped(weights):
    return jnp.transpose(weights[::-1], (0, 2, 1))


def on_device(column_features, column_route, cotangent, first_weight, second_weight):
    count_x = lax.axis_size("rx")
    count_y = lax.axis_size("ry")
    count_all = count_x * count_y
    shard_rows = column_features.shape[0]
    row_width = column_features.shape[1]
    region_x = cotangent.shape[0]
    region_y = cotangent.shape[1]
    channels = first_weight.shape[1]
    depth = row_width // channels
    region_slots = region_x * region_y
    capacity = 2 * shard_rows // count_all
    owners = column_route // region_slots
    slot_ids = column_route % region_slots
    shard_index = jnp.arange(shard_rows, dtype=jnp.int32)
    earlier = shard_index[:, None] > shard_index[None, :]
    same_owner = owners[:, None] == owners[None, :]
    ranks = jnp.sum(jnp.logical_and(earlier, same_owner).astype(jnp.int32), axis=1)
    send_pos = owners * capacity + ranks
    buffer_index = jnp.arange(count_all * capacity, dtype=jnp.int32)
    send_hot = send_pos[:, None] == buffer_index[None, :]
    send_table = send_hot.astype(jnp.bfloat16)
    outgoing = jnp.einsum(
        "sr,sw->rw", send_table, column_features, preferred_element_type=jnp.float32
    ).astype(jnp.bfloat16)
    filled = jnp.sum(send_hot.astype(jnp.int32), axis=0)
    slot_total = jnp.sum(jnp.where(send_hot, slot_ids[:, None], 0), axis=0)
    out_slots = jnp.where(filled > 0, slot_total, region_slots)
    incoming, in_slots = (
        lax.all_to_all(
            outgoing.reshape(count_all, capacity, row_width),
            ("rx", "ry"),
            split_axis=0,
            concat_axis=0,
            tiled=True,
        ),
        lax.all_to_all(
            out_slots.reshape(count_all, capacity),
            ("rx", "ry"),
            split_axis=0,
            concat_axis=0,
            tiled=True,
        ),
    )
    incoming = incoming.reshape(count_all * capacity, row_width)
    in_slots = in_slots.reshape(count_all * capacity)
    slot_hot = in_slots[:, None] == jnp.arange(region_slots, dtype=jnp.int32)[None, :]
    slot_table = slot_hot.astype(jnp.bfloat16)
    region_rows = jnp.einsum(
        "rs,rw->sw", slot_table, incoming, preferred_element_type=jnp.float32
    ).astype(jnp.bfloat16)
    active = jnp.sum(slot_hot.astype(jnp.float32), axis=0)
    field = jnp.transpose(region_rows.reshape(region_x, region_y, channels, depth), (0, 1, 3, 2))
    mask = active.reshape(region_x, region_y, 1, 1)
    cot_field = jnp.transpose(
        cotangent.reshape(region_x, region_y, channels, depth), (0, 1, 3, 2)
    ).astype(jnp.float32)
    outer_grad = (mask * cot_field).astype(jnp.bfloat16)
    field_flat = field.reshape(region_x, region_y, row_width)
    outer_flat = outer_grad.reshape(region_x, region_y, row_width)
    padded_x = pad_depth(extended(field_flat, (("rx", 0), ("ry", 1)), 1), channels)
    padded_g = pad_depth(extended(outer_flat, (("rx", 0), ("ry", 1)), 1), channels)
    hidden = mask * conv_sum(padded_x, first_weight)
    act = jax.nn.silu(hidden).astype(jnp.bfloat16)
    padded_a = face_field(act.reshape(region_x, region_y, row_width), channels)
    second = conv_sum(padded_a, second_weight)
    summed = (field.astype(jnp.float32) + mask * second).astype(jnp.bfloat16)
    block_output = jnp.transpose(summed, (0, 1, 3, 2)).reshape(region_x, region_y, row_width)
    act_grad = conv_sum(padded_g, flipped(second_weight))
    sigma = jax.nn.sigmoid(hidden)
    hidden_grad = (mask * act_grad * sigma * (1.0 + hidden * (1.0 - sigma))).astype(jnp.bfloat16)
    padded_h = face_field(hidden_grad.reshape(region_x, region_y, row_width), channels)
    grid_grad = (mask * cot_field + conv_sum(padded_h, flipped(first_weight))).astype(jnp.bfloat16)
    grad_rows = jnp.transpose(grid_grad, (0, 1, 3, 2)).reshape(region_slots, row_width)
    backward = jnp.dot(slot_table, grad_rows, preferred_element_type=jnp.float32).astype(
        jnp.bfloat16
    )
    returned = lax.all_to_all(
        backward.reshape(count_all, capacity, row_width),
        ("rx", "ry"),
        split_axis=0,
        concat_axis=0,
        tiled=True,
    )
    returned_rows = returned.reshape(count_all * capacity, row_width)
    feature_grads = jnp.dot(send_table, returned_rows, preferred_element_type=jnp.float32).astype(
        jnp.bfloat16
    )
    second_local = correlate(outer_grad, padded_a)
    first_local = correlate(hidden_grad, padded_x)
    first_total, second_total = lax.psum((first_local, second_local), ("rx", "ry"))
    factor = 1.0 / jnp.sqrt(jnp.float32(count_all * shard_rows * depth))
    return (block_output, feature_grads, first_total * factor, second_total * factor)


def solution(mesh):
    in_specs = (P(("rx", "ry"), None), P(("rx", "ry")), P("rx", "ry", None), P(), P())
    out_specs = (P("rx", "ry", None), P(("rx", "ry"), None), P(), P())
    return jax.shard_map(
        on_device, mesh=mesh, in_specs=in_specs, out_specs=out_specs, check_vma=False
    )
```

profile of v0, /device:TPU:1, one launch (start us, length us, event | category | flops | bytes accessed | tf_op | source)
XLA Modules:
  0.0 670.0 jit_solution(15882649967225699093)
XLA Ops:
  9.0 11.5 %all-to-all-start = ((s32[128,1,2]{2,1,0:T(1,128)}), s32[128,1,2]{2,1,0:T(1,128)S(1)}, u32[]{:S(2)}, u32[]{:S(2)}) async-start(s32[128,1,2]{2,1,0:T(1,128)} %bitcast), calls=%async_computation | async-start | bytes 131072 | tf_op jit(solution)/shard_map/all_to_all | solution.py:103
  24.4 6.9 %reshape.118 = f32[16,16,96,16]{3,2,1,0:T(8,128)} reshape(bf16[16,16,1536]{2,1,0:T(8,128)(2,1)S(1)} %copy-done.16) | data formatting | bytes 2359296 | tf_op jit(solution)/shard_map/convert_element_type | solution.py:123
  31.2 8.4 %copy.37 = f32[16,16,96,16]{2,3,1,0:T(8,128)S(1)} copy(f32[16,16,96,16]{3,2,1,0:T(8,128)} %reshape.118) | data formatting | bytes 3145728 | tf_op jit(solution)/shard_map/convert_element_type | solution.py:123
  39.7 10.2 %all-to-all-start.1 = ((bf16[128,2,1536]{2,1,0:T(2,128)(2,1)}), bf16[128,2,1536]{2,1,0:T(2,128)(2,1)}, u32[]{:S(2)}, u32[]{:S(2)}) async-start(bf16[128,2,1536]{2,1,0:T(2,128)(2,1)} %reshape.103), calls=%async_computation.1 | async-start | bytes 1572864 | tf_op jit(solution)/shard_map/all_to_all | solution.py:96
  52.0 3.5 collective-permute-start.8
  62.3 3.8 collective-permute-done.9
  66.3 3.1 collective-permute-start.10
  71.8 3.1 collective-permute-done.11
  123.2 6.8 %reshape.105 = bf16[16,16,96,16]{3,2,1,0:T(8,128)(2,1)} reshape(bf16[256,1536]{1,0:T(8,128)(2,1)S(1)} %convolution_convert_fusion.2) | data formatting | bytes 1572864 | tf_op jit(solution)/shard_map/reshape | solution.py:119
  132.0 3.9 collective-permute-start
  138.5 6.0 copy.34
  150.5 3.4 collective-permute-start.2
  157.7 6.1 copy.32
  165.5 2.7 reshape.107
  168.3 2.6 fusion.114
  215.7 20.1 %multiply_convert_fusion.1 = (bf16[16,16,16,96]{3,2,1,0:T(8,128)(2,1)}, f32[16,16,16,96]{3,2,1,0:T(8,128)}) fusion(bf16[27,96,96]{2,1,0:T(8,128)(2,1)} %param.8, bf16[18,18,16,96]{3,2,1,0:T(8,128)(2,1)S(1)} %reshape.107, f32[16,16,16,96]{3,2,1,0:T(8,128)} %fusion.208, f32[16,16,16,96]{3,2,1,0:T(8,128)} %fusion.129, f32[16,16,16,96]{3,2,1,0:T(8,128)} %fusion.128, ...), kind=kOutput, calls=%fused_computation.102 | convolution fusion | flops 88080384 | bytes 57906176 | tf_op jit(solution)/shard_map/xyzi,oi->xyzo/dot_general | solution.py:41
  235.8 20.1 %multiply_convert_fusion = bf16[16,16,16,96]{3,2,1,0:T(8,128)(2,1)} fusion(f32[16,16,16,96]{3,2,1,0:T(8,128)} %get-tuple-element.27, f32[16,16,16,96]{3,2,1,0:T(8,128)} %fusion.162, f32[16,16,16,96]{3,2,1,0:T(8,128)} %fusion.76, f32[16,16,16,96]{3,2,1,0:T(8,128)} %fusion.75, f32[16,16,16,96]{3,2,1,0:T(8,128)} %fusion.163, f32[16,16,16,96]{3,2,1,0:T(8,128)} %fusion.74, ...), kind=kOutput, calls=%fused_computation.101 | convolution fusion | flops 89653248 | bytes 58430464 | tf_op jit(solution)/shard_map/xyzi,oi->xyzo/dot_general | solution.py:41
  262.0 3.2 collective-permute-start.12
  304.0 4.0 collective-permute-start.6
  309.6 4.9 collective-permute-start.14
  317.6 2.6 fusion.132
  367.8 2.9 reshape.114
  370.7 2.6 fusion.79
  447.1 19.9 %fusion.1 = bf16[16,16,96,16]{2,3,1,0:T(8,128)(2,1)} fusion(f32[16,16,16,96]{3,2,1,0:T(8,128)} %fusion.153, f32[16,16,16,96]{3,2,1,0:T(8,128)} %fusion.94, f32[16,16,16,96]{3,2,1,0:T(8,128)} %fusion.93, f32[16,16,16,96]{3,2,1,0:T(8,128)} %fusion.154, f32[16,16,16,96]{3,2,1,0:T(8,128)} %fusion.92, f32[16,16,16,96]{3,2,1,0:T(8,128)} %fusion.91, ...), kind=kOutput, calls=%fused_computation.78 | convolution fusion | flops 86900736 | bytes 58430464 | tf_op jit(solution)/shard_map/xyzi,oi->xyzo/dot_general | solution.py:41
  466.9 6.0 copy.40
  472.9 11.3 %reshape.115 = bf16[256,1536]{1,0:T(8,128)(2,1)S(1)} reshape(bf16[16,16,96,16]{3,2,1,0:T(8,128)(2,1)} %copy.40) | data formatting | bytes 1572864 | tf_op jit(solution)/shard_map/reshape | solution.py:140
  485.9 13.1 %all-to-all-start.2 = ((bf16[128,2,1536]{2,1,0:T(2,128)(2,1)}), bf16[128,2,1536]{2,1,0:T(2,128)(2,1)S(1)}, u32[]{:S(2)}, u32[]{:S(2)}) async-start(bf16[128,2,1536]{2,1,0:T(2,128)(2,1)} %reshape.116), calls=%async_computation.2 | async-start | bytes 1572864 | tf_op jit(solution)/shard_map/all_to_all | solution.py:144
  499.8 19.6 %fusion.4 = bf16[16,16,96,16]{2,3,1,0:T(8,128)(2,1)} fusion(f32[16,16,16,96]{3,2,1,0:T(8,128)} %fusion.172, f32[16,16,16,96]{3,2,1,0:T(8,128)} %fusion.147, f32[16,16,16,96]{3,2,1,0:T(8,128)} %fusion.146, f32[16,16,16,96]{3,2,1,0:T(8,128)} %fusion.176, f32[16,16,16,96]{3,2,1,0:T(8,128)} %fusion.145, f32[16,16,16,96]{3,2,1,0:T(8,128)} %fusion.144, ...), kind=kOutput, calls=%fused_computation.91 | convolution fusion | flops 87293952 | bytes 57119744 | tf_op jit(solution)/shard_map/xyzi,oi->xyzo/dot_general | solution.py:41
  519.4 6.0 copy.36
  525.4 11.8 %reshape.110 = bf16[16,16,1536]{2,1,0:T(8,128)(2,1)} reshape(bf16[16,16,96,16]{3,2,1,0:T(8,128)(2,1)} %copy.36) | data formatting | bytes 1572864 | tf_op jit(solution)/shard_map/reshape | solution.py:134
  538.6 120.6 %all-reduce.7.cloned.1.call-done = (f32[27,96,96]{2,1,0:T(8,128)}, f32[27,96,96]{2,1,0:T(8,128)}) async-done(((f32[27,96,96]{2,1,0:T(8,128)}, f32[27,96,96]{2,1,0:T(8,128)}), (f32[27,96,96]{2,1,0:T(8,128)}, f32[27,96,96]{2,1,0:T(8,128)})) %all-reduce.7.cloned.1.call-update) | async-done | bytes 1990672 | tf_op jit(solution)/shard_map/psum | solution.py:157
  659.2 3.5 broadcast_multiply_fusion
  (293 shorter events, 300.5 us)
Async XLA Ops:
  7.2 13.3 %copy-start = (bf16[128,1536]{1,0:T(8,128)(2,1)S(1)}, bf16[128,1536]{1,0:T(8,128)(2,1)}, u32[]{:S(2)}) copy-start(bf16[128,1536]{1,0:T(8,128)(2,1)} %param.5) | copy-start | bytes 1179652
  8.1 16.3 %copy-start.21 = (s32[128]{0:T(128)}, s32[128]{0:T(128)S(1)}, u32[]{:S(2)}) copy-start(s32[128]{0:T(128)S(1)} %multiply_add_fusion) | copy-start | bytes 1540
  9.0 30.7 %all-to-all-start = ((s32[128,1,2]{2,1,0:T(1,128)}), s32[128,1,2]{2,1,0:T(1,128)S(1)}, u32[]{:S(2)}, u32[]{:S(2)}) async-start(s32[128,1,2]{2,1,0:T(1,128)} %bitcast), calls=%async_computation | async-start | bytes 131072 | tf_op jit(solution)/shard_map/all_to_all | solution.py:103
  20.5 3.8 copy-start.16
  39.6 12.2 %copy-start.2 = (f32[16,16,96,16]{2,3,1,0:T(8,128)}, f32[16,16,96,16]{2,3,1,0:T(8,128)S(1)}, u32[]{:S(2)}) copy-start(f32[16,16,96,16]{2,3,1,0:T(8,128)S(1)} %copy.37) | copy-start | bytes 4718596
  39.7 80.8 %all-to-all-start.1 = ((bf16[128,2,1536]{2,1,0:T(2,128)(2,1)}), bf16[128,2,1536]{2,1,0:T(2,128)(2,1)}, u32[]{:S(2)}, u32[]{:S(2)}) async-start(bf16[128,2,1536]{2,1,0:T(2,128)(2,1)} %reshape.103), calls=%async_computation.1 | async-start | bytes 1572864 | tf_op jit(solution)/shard_map/all_to_all | solution.py:96
  51.3 71.4 %copy-start.19 = (s32[256]{0:T(256)}, s32[256]{0:T(256)S(1)}, u32[]{:S(2)}) copy-start(s32[256]{0:T(256)S(1)} %eq.49) | copy-start | bytes 3076
  51.5 6.0 copy-start.17
  51.9 8.3 %copy-start.6 = (bf16[16,16,16,96]{3,2,1,0:T(8,128)(2,1)}, bf16[16,16,16,96]{3,2,1,0:T(8,128)(2,1)S(1)}, u32[]{:S(2)}) copy-start(bf16[16,16,16,96]{3,2,1,0:T(8,128)(2,1)S(1)} %fusion.59) | copy-start | bytes 2359300
  52.0 10.2 %collective-permute-start.8 = (bf16[1,16,1536]{2,1,0:T(8,128)(2,1)S(1)}, bf16[1,16,1536]{2,1,0:T(8,128)(2,1)S(1)}, u32[]{:S(2)}, u32[]{:S(2)}) collective-permute-start(bf16[1,16,1536]{2,1,0:T(8,128)(2,1)S(1)} %slice.931), channel_id=1, source_target_pairs={{0,16},{16,32},{32,48},{48,64},{64,80},{80,96},{96,112},{1,17},{17... | collective-permute-start | bytes 147464 | tf_op jit(solution)/shard_map/ppermute | solution.py:12
  60.3 5.8 collective-permute-start.9
  66.3 5.5 collective-permute-start.10
  69.4 5.5 collective-permute-start.11
  132.0 16.0 %collective-permute-start = (bf16[1,16,1536]{2,1,0:T(8,128)(2,1)}, bf16[1,16,1536]{2,1,0:T(8,128)(2,1)}, u32[]{:S(2)}, u32[]{:S(2)}) collective-permute-start(bf16[1,16,1536]{2,1,0:T(8,128)(2,1)} %slice.811), channel_id=1, source_target_pairs={{0,16},{16,32},{32,48},{48,64},{64,80},{80,96},{96,112},{1,17},{17... | collective-permute-start | bytes 147464 | tf_op jit(solution)/shard_map/ppermute | solution.py:12
  144.9 5.4 collective-permute-start.1
  150.5 13.3 %collective-permute-start.2 = (bf16[18,1,1536]{2,1,0:T(2,128)(2,1)S(1)}, bf16[18,1,1536]{2,1,0:T(2,128)(2,1)S(1)}, u32[]{:S(2)}, u32[]{:S(2)}) collective-permute-start(bf16[18,1,1536]{2,1,0:T(2,128)(2,1)S(1)} %get-tuple-element.22), channel_id=1, source_target_pairs={{0,1},{1,2},{2,3},{3,4},{4,5},{5,6},{6,7},{7,8},{8,9},{9,10},{10,1... | collective-permute-start | bytes 165896 | tf_op jit(solution)/shard_map/ppermute | solution.py:12
  153.8 10.0 %collective-permute-start.3 = (bf16[18,1,1536]{2,1,0:T(2,128)(2,1)S(1)}, bf16[18,1,1536]{2,1,0:T(2,128)(2,1)S(1)}, u32[]{:S(2)}, u32[]{:S(2)}) collective-permute-start(bf16[18,1,1536]{2,1,0:T(2,128)(2,1)S(1)} %get-tuple-element.23), channel_id=1, source_target_pairs={{1,0},{2,1},{3,2},{4,3},{5,4},{6,5},{7,6},{8,7},{9,8},{10,9},{11,1... | collective-permute-start | bytes 165896 | tf_op jit(solution)/shard_map/ppermute | solution.py:15
  259.4 43.0 %collective-permute-start.4 = (bf16[1,16,1536]{2,1,0:T(8,128)(2,1)S(1)}, bf16[1,16,1536]{2,1,0:T(8,128)(2,1)S(1)}, u32[]{:S(2)}, u32[]{:S(2)}) collective-permute-start(bf16[1,16,1536]{2,1,0:T(8,128)(2,1)S(1)} %slice.871), channel_id=1, source_target_pairs={{0,16},{16,32},{32,48},{48,64},{64,80},{80,96},{96,112},{1,17},{17... | collective-permute-start | bytes 147464 | tf_op jit(solution)/shard_map/ppermute | solution.py:12
  262.0 5.5 copy-start.4
  262.0 47.2 %collective-permute-start.12 = (bf16[1,16,1536]{2,1,0:T(8,128)(2,1)S(1)}, bf16[1,16,1536]{2,1,0:T(8,128)(2,1)S(1)}, u32[]{:S(2)}, u32[]{:S(2)}) collective-permute-start(bf16[1,16,1536]{2,1,0:T(8,128)(2,1)S(1)} %slice.991), channel_id=1, source_target_pairs={{0,16},{16,32},{32,48},{48,64},{64,80},{80,96},{96,112},{1,17},{17... | collective-permute-start | bytes 147464 | tf_op jit(solution)/shard_map/ppermute | solution.py:12
  298.4 5.4 collective-permute-start.5
  300.4 8.9 %collective-permute-start.13 = (bf16[1,16,1536]{2,1,0:T(8,128)(2,1)S(1)}, bf16[1,16,1536]{2,1,0:T(8,128)(2,1)S(1)}, u32[]{:S(2)}, u32[]{:S(2)}) collective-permute-start(bf16[1,16,1536]{2,1,0:T(8,128)(2,1)S(1)} %slice.993), channel_id=1, source_target_pairs={{16,0},{32,16},{48,32},{64,48},{80,64},{96,80},{112,96},{17,1},{33... | collective-permute-start | bytes 147464 | tf_op jit(solution)/shard_map/ppermute | solution.py:15
  304.0 11.8 %collective-permute-start.6 = (bf16[18,1,1536]{2,1,0:T(2,128)(2,1)S(1)}, bf16[18,1,1536]{2,1,0:T(2,128)(2,1)S(1)}, u32[]{:S(2)}, u32[]{:S(2)}) collective-permute-start(bf16[18,1,1536]{2,1,0:T(2,128)(2,1)S(1)} %get-tuple-element.20), channel_id=1, source_target_pairs={{0,1},{1,2},{2,3},{3,4},{4,5},{5,6},{6,7},{7,8},{8,9},{9,10},{10,1... | collective-permute-start | bytes 165896 | tf_op jit(solution)/shard_map/ppermute | solution.py:12
  308.0 7.8 %collective-permute-start.7 = (bf16[18,1,1536]{2,1,0:T(2,128)(2,1)S(1)}, bf16[18,1,1536]{2,1,0:T(2,128)(2,1)S(1)}, u32[]{:S(2)}, u32[]{:S(2)}) collective-permute-start(bf16[18,1,1536]{2,1,0:T(2,128)(2,1)S(1)} %get-tuple-element.21), channel_id=1, source_target_pairs={{1,0},{2,1},{3,2},{4,3},{5,4},{6,5},{7,6},{8,7},{9,8},{10,9},{11,1... | collective-permute-start | bytes 165896 | tf_op jit(solution)/shard_map/ppermute | solution.py:15
  309.4 6.4 copy-start.14
  309.6 56.5 %collective-permute-start.14 = (bf16[18,1,1536]{2,1,0:T(2,128)(2,1)S(1)}, bf16[18,1,1536]{2,1,0:T(2,128)(2,1)S(1)}, u32[]{:S(2)}, u32[]{:S(2)}) collective-permute-start(bf16[18,1,1536]{2,1,0:T(2,128)(2,1)S(1)} %get-tuple-element.16), channel_id=1, source_target_pairs={{0,1},{1,2},{2,3},{3,4},{4,5},{5,6},{6,7},{7,8},{8,9},{9,10},{10,1... | collective-permute-start | bytes 165896 | tf_op jit(solution)/shard_map/ppermute | solution.py:12
  314.4 51.6 %collective-permute-start.15 = (bf16[18,1,1536]{2,1,0:T(2,128)(2,1)S(1)}, bf16[18,1,1536]{2,1,0:T(2,128)(2,1)S(1)}, u32[]{:S(2)}, u32[]{:S(2)}) collective-permute-start(bf16[18,1,1536]{2,1,0:T(2,128)(2,1)S(1)} %get-tuple-element.17), channel_id=1, source_target_pairs={{1,0},{2,1},{3,2},{4,3},{5,4},{6,5},{7,6},{8,7},{9,8},{10,9},{11,1... | collective-permute-start | bytes 165896 | tf_op jit(solution)/shard_map/ppermute | solution.py:15
  472.9 11.3 %copy-start.20 = (s32[256]{0:T(256)S(1)}, s32[256]{0:T(256)}, u32[]{:S(2)}) copy-start(s32[256]{0:T(256)} %copy-done.19) | copy-start | bytes 3076
  485.9 13.9 %copy-start.9 = (bf16[16,16,96,16]{2,3,1,0:T(8,128)(2,1)S(1)}, bf16[16,16,96,16]{2,3,1,0:T(8,128)(2,1)}, u32[]{:S(2)}) copy-start(bf16[16,16,96,16]{2,3,1,0:T(8,128)(2,1)} %copy.32) | copy-start | bytes 2359300
  485.9 51.3 %all-to-all-start.2 = ((bf16[128,2,1536]{2,1,0:T(2,128)(2,1)}), bf16[128,2,1536]{2,1,0:T(2,128)(2,1)S(1)}, u32[]{:S(2)}, u32[]{:S(2)}) async-start(bf16[128,2,1536]{2,1,0:T(2,128)(2,1)} %reshape.116), calls=%async_computation.2 | async-start | bytes 1572864 | tf_op jit(solution)/shard_map/all_to_all | solution.py:144
  499.0 160.2 %all-reduce.7.cloned.1.call-start = ((), (), s32[]{:S(2)}) async-start(), calls=%async_computation.3 | async-start | bytes 5308416 | tf_op jit(solution)/shard_map/psum | solution.py:157
  525.4 12.1 %copy-start.22 = (s32[128]{0:T(128)S(1)}, s32[128]{0:T(128)}, u32[]{:S(2)}) copy-start(s32[128]{0:T(128)} %copy-done.21) | copy-start | bytes 1540
  (11 other events, 24.8 us)
Sparse Core Ops, SparseCore 0:
  505.5 153.6 all-reduce.6
where the time goes:
time: 677 us; the launch traced here: 670 us
  matrix products  336 us (50%)
  waiting for transfers between devices  131 us (19%)
  local copies, waits for them, and re-layouts  101 us (15%)
  starting transfers between devices  76.5 us (11%)
  between operations  15.2 us (2%)
  other arithmetic  10.5 us (2%)
    dot_general x108, matrix products, conv_sum(): jnp.einsum('xyzi,oi->xyzo', piece, weights[9 * a + 3 * b + c], preferred_...  270 us
    psum x1, waiting for transfers between devices, on_device(): lax.psum((first_local, second_local), ('rx', 'ry'))  121 us
    dot_general x54, matrix products, correlate(): jnp.einsum('xyzo,xyzi->oi', grads, piece, preferred_element_type=jnp.floa...  63.1 us
    ppermute x8, starting transfers between devices, extended(): lax.ppermute(lax.slice_in_dim(block, block.shape[dim] - width, None, axis...  28.5 us
    convert_element_type x2, local copies, waits for them, and re-layouts, on_device(): cot_field = jnp.transpose(cotangent.reshape(region_x, region_y, channels,...  15.3 us
  transfers between devices with their start and end apart: 20, of which 5 were waited for; matrix products, arithmetic and copies ran while one was open for 32% of the time, Pallas kernels for 0%

commit v1 on v0

--- a/solution.py
+++ b/solution.py
@@ -154,7 +154,7 @@
     )
     second_local = correlate(outer_grad, padded_a)
     first_local = correlate(hidden_grad, padded_x)
-    first_total, second_total = lax.psum((first_local, second_local), ("rx", "ry"))
+    first_total, second_total = lax.psum(lax.psum((first_local, second_local), "rx"), "ry")
     factor = 1.0 / jnp.sqrt(jnp.float32(count_all * shard_rows * depth))
     return (block_output, feature_grads, first_total * factor, second_total * factor)
 

time: 677 us -> 672 us (level)
  waiting for transfers between devices: 131 us -> 122 us
    psum x1 -> x2, waiting for transfers between devices: 121 us -> 112 us  [the longest x1 58.9 us: on_device(): lax.psum(lax.psum((first_local, second_local), 'rx'), 'ry')]
  transfers between devices with their start and end apart: 20 -> 21, of which waited for: 5 -> 6; matrix products, arithmetic and copies ran while one was open for 32% -> 33% of each run, Pallas kernels for 0% -> 0%
where the time goes in v1:
time: 672 us; the launch traced here: 664 us
  matrix products  338 us (50%)
  waiting for transfers between devices  122 us (18%)
  local copies, waits for them, and re-layouts  102 us (15%)
  starting transfers between devices  76.5 us (11%)
  between operations  15.3 us (2%)
  other arithmetic  10.5 us (2%)
    dot_general x108, matrix products, conv_sum(): jnp.einsum('xyzi,oi->xyzo', piece, weights[9 * a + 3 * b + c], preferred_...  273 us
    dot_general x54, matrix products, correlate(): jnp.einsum('xyzo,xyzi->oi', grads, piece, preferred_element_type=jnp.floa...  63.1 us
    psum x1, waiting for transfers between devices, on_device(): lax.psum(lax.psum((first_local, second_local), 'rx'), 'ry')  58.9 us
    psum x1, waiting for transfers between devices, on_device(): lax.psum((first_local, second_local), 'rx')  53.4 us
    ppermute x8, starting transfers between devices, extended(): lax.ppermute(lax.slice_in_dim(block, block.shape[dim] - width, None, axis...  28.6 us
    convert_element_type x2, local copies, waits for them, and re-layouts, on_device(): cot_field = jnp.transpose(cotangent.reshape(region_x, region_y, channels,...  15.3 us
  transfers between devices with their start and end apart: 21, of which 6 were waited for; matrix products, arithmetic and copies ran while one was open for 33% of the time, Pallas kernels for 0%

profile of v1, /device:TPU:1, one launch (start us, length us, event | category | flops | bytes accessed | tf_op | source)
XLA Modules:
  0.0 664.2 jit_solution(17765415442161282830)
XLA Ops:
  9.0 11.5 %all-to-all-start = ((s32[128,1,2]{2,1,0:T(1,128)}), s32[128,1,2]{2,1,0:T(1,128)S(1)}, u32[]{:S(2)}, u32[]{:S(2)}) async-start(s32[128,1,2]{2,1,0:T(1,128)} %bitcast), calls=%async_computation | async-start | bytes 131072 | tf_op jit(solution)/shard_map/all_to_all | solution.py:103
  24.4 6.9 %reshape.118 = f32[16,16,96,16]{3,2,1,0:T(8,128)} reshape(bf16[16,16,1536]{2,1,0:T(8,128)(2,1)S(1)} %copy-done.16) | data formatting | bytes 2359296 | tf_op jit(solution)/shard_map/convert_element_type | solution.py:123
  31.2 8.4 %copy.37 = f32[16,16,96,16]{2,3,1,0:T(8,128)S(1)} copy(f32[16,16,96,16]{3,2,1,0:T(8,128)} %reshape.118) | data formatting | bytes 3145728 | tf_op jit(solution)/shard_map/convert_element_type | solution.py:123
  39.7 10.2 %all-to-all-start.1 = ((bf16[128,2,1536]{2,1,0:T(2,128)(2,1)}), bf16[128,2,1536]{2,1,0:T(2,128)(2,1)}, u32[]{:S(2)}, u32[]{:S(2)}) async-start(bf16[128,2,1536]{2,1,0:T(2,128)(2,1)} %reshape.103), calls=%async_computation.1 | async-start | bytes 1572864 | tf_op jit(solution)/shard_map/all_to_all | solution.py:96
  52.1 3.5 collective-permute-start.8
  62.4 3.8 collective-permute-done.9
  66.4 3.0 collective-permute-start.10
  71.8 3.1 collective-permute-done.11
  123.2 6.7 %reshape.105 = bf16[16,16,96,16]{3,2,1,0:T(8,128)(2,1)} reshape(bf16[256,1536]{1,0:T(8,128)(2,1)S(1)} %convolution_convert_fusion.2) | data formatting | bytes 1572864 | tf_op jit(solution)/shard_map/reshape | solution.py:119
  132.0 4.0 collective-permute-start
  138.6 6.0 copy.34
  150.5 3.4 collective-permute-start.2
  157.8 6.2 copy.32
  165.6 2.7 reshape.107
  168.4 2.6 fusion.114
  215.7 20.1 %multiply_convert_fusion.1 = (bf16[16,16,16,96]{3,2,1,0:T(8,128)(2,1)}, f32[16,16,16,96]{3,2,1,0:T(8,128)}) fusion(bf16[27,96,96]{2,1,0:T(8,128)(2,1)} %param.8, bf16[18,18,16,96]{3,2,1,0:T(8,128)(2,1)S(1)} %reshape.107, f32[16,16,16,96]{3,2,1,0:T(8,128)} %fusion.208, f32[16,16,16,96]{3,2,1,0:T(8,128)} %fusion.129, f32[16,16,16,96]{3,2,1,0:T(8,128)} %fusion.128, ...), kind=kOutput, calls=%fused_computation.102 | convolution fusion | flops 88080384 | bytes 57906176 | tf_op jit(solution)/shard_map/xyzi,oi->xyzo/dot_general | solution.py:41
  235.8 20.1 %multiply_convert_fusion = bf16[16,16,16,96]{3,2,1,0:T(8,128)(2,1)} fusion(f32[16,16,16,96]{3,2,1,0:T(8,128)} %get-tuple-element.29, f32[16,16,16,96]{3,2,1,0:T(8,128)} %fusion.162, f32[16,16,16,96]{3,2,1,0:T(8,128)} %fusion.76, f32[16,16,16,96]{3,2,1,0:T(8,128)} %fusion.75, f32[16,16,16,96]{3,2,1,0:T(8,128)} %fusion.163, f32[16,16,16,96]{3,2,1,0:T(8,128)} %fusion.74, ...), kind=kOutput, calls=%fused_computation.101 | convolution fusion | flops 89653248 | bytes 58430464 | tf_op jit(solution)/shard_map/xyzi,oi->xyzo/dot_general | solution.py:41
  262.1 3.2 collective-permute-start.12
  304.0 4.0 collective-permute-start.6
  309.6 4.9 collective-permute-start.14
  362.4 2.9 reshape.114
  365.3 2.6 fusion.79
  441.7 20.0 %fusion.1 = bf16[16,16,96,16]{2,3,1,0:T(8,128)(2,1)} fusion(f32[16,16,16,96]{3,2,1,0:T(8,128)} %fusion.153, f32[16,16,16,96]{3,2,1,0:T(8,128)} %fusion.94, f32[16,16,16,96]{3,2,1,0:T(8,128)} %fusion.93, f32[16,16,16,96]{3,2,1,0:T(8,128)} %fusion.154, f32[16,16,16,96]{3,2,1,0:T(8,128)} %fusion.92, f32[16,16,16,96]{3,2,1,0:T(8,128)} %fusion.91, ...), kind=kOutput, calls=%fused_computation.78 | convolution fusion | flops 86900736 | bytes 58430464 | tf_op jit(solution)/shard_map/xyzi,oi->xyzo/dot_general | solution.py:41
  461.6 6.0 copy.40
  467.6 11.3 %reshape.115 = bf16[256,1536]{1,0:T(8,128)(2,1)S(1)} reshape(bf16[16,16,96,16]{3,2,1,0:T(8,128)(2,1)} %copy.40) | data formatting | bytes 1572864 | tf_op jit(solution)/shard_map/reshape | solution.py:140
  481.2 13.2 %all-to-all-start.2 = ((bf16[128,2,1536]{2,1,0:T(2,128)(2,1)}), bf16[128,2,1536]{2,1,0:T(2,128)(2,1)S(1)}, u32[]{:S(2)}, u32[]{:S(2)}) async-start(bf16[128,2,1536]{2,1,0:T(2,128)(2,1)} %reshape.116), calls=%async_computation.2 | async-start | bytes 1572864 | tf_op jit(solution)/shard_map/all_to_all | solution.py:144
  502.0 53.4 %all-reduce.11.cloned.1.call-done = (f32[27,96,96]{2,1,0:T(8,128)}, f32[27,96,96]{2,1,0:T(8,128)}) async-done(((f32[27,96,96]{2,1,0:T(8,128)}, f32[27,96,96]{2,1,0:T(8,128)}), (f32[27,96,96]{2,1,0:T(8,128)}, f32[27,96,96]{2,1,0:T(8,128)})) %all-reduce.11.cloned.1.call-update) | async-done | bytes 1990672 | tf_op jit(solution)/shard_map/psum | solution.py:157
  555.5 19.9 %fusion.4 = bf16[16,16,96,16]{2,3,1,0:T(8,128)(2,1)} fusion(f32[16,16,16,96]{3,2,1,0:T(8,128)} %fusion.172, f32[16,16,16,96]{3,2,1,0:T(8,128)} %fusion.147, f32[16,16,16,96]{3,2,1,0:T(8,128)} %fusion.146, f32[16,16,16,96]{3,2,1,0:T(8,128)} %fusion.176, f32[16,16,16,96]{3,2,1,0:T(8,128)} %fusion.145, f32[16,16,16,96]{3,2,1,0:T(8,128)} %fusion.144, ...), kind=kOutput, calls=%fused_computation.91 | convolution fusion | flops 87293952 | bytes 57119744 | tf_op jit(solution)/shard_map/xyzi,oi->xyzo/dot_general | solution.py:41
  575.4 6.0 copy.36
  581.4 11.8 %reshape.110 = bf16[16,16,1536]{2,1,0:T(8,128)(2,1)} reshape(bf16[16,16,96,16]{3,2,1,0:T(8,128)(2,1)} %copy.36) | data formatting | bytes 1572864 | tf_op jit(solution)/shard_map/reshape | solution.py:134
  594.5 58.9 %all-reduce.9.cloned.1.call-done = (f32[27,96,96]{2,1,0:T(8,128)}, f32[27,96,96]{2,1,0:T(8,128)}) async-done(((f32[27,96,96]{2,1,0:T(8,128)}, f32[27,96,96]{2,1,0:T(8,128)}), (f32[27,96,96]{2,1,0:T(8,128)}, f32[27,96,96]{2,1,0:T(8,128)})) %all-reduce.9.cloned.1.call-update) | async-done | bytes 1990672 | tf_op jit(solution)/shard_map/psum | solution.py:157
  653.4 3.5 broadcast_multiply_fusion
  (296 shorter events, 305.2 us)
Async XLA Ops:
  7.2 13.3 %copy-start = (bf16[128,1536]{1,0:T(8,128)(2,1)S(1)}, bf16[128,1536]{1,0:T(8,128)(2,1)}, u32[]{:S(2)}) copy-start(bf16[128,1536]{1,0:T(8,128)(2,1)} %param.5) | copy-start | bytes 1179652
  8.1 16.3 %copy-start.21 = (s32[128]{0:T(128)}, s32[128]{0:T(128)S(1)}, u32[]{:S(2)}) copy-start(s32[128]{0:T(128)S(1)} %multiply_add_fusion) | copy-start | bytes 1540
  9.0 30.7 %all-to-all-start = ((s32[128,1,2]{2,1,0:T(1,128)}), s32[128,1,2]{2,1,0:T(1,128)S(1)}, u32[]{:S(2)}, u32[]{:S(2)}) async-start(s32[128,1,2]{2,1,0:T(1,128)} %bitcast), calls=%async_computation | async-start | bytes 131072 | tf_op jit(solution)/shard_map/all_to_all | solution.py:103
  20.5 3.8 copy-start.16
  39.7 12.3 %copy-start.2 = (f32[16,16,96,16]{2,3,1,0:T(8,128)}, f32[16,16,96,16]{2,3,1,0:T(8,128)S(1)}, u32[]{:S(2)}) copy-start(f32[16,16,96,16]{2,3,1,0:T(8,128)S(1)} %copy.37) | copy-start | bytes 4718596
  39.7 80.8 %all-to-all-start.1 = ((bf16[128,2,1536]{2,1,0:T(2,128)(2,1)}), bf16[128,2,1536]{2,1,0:T(2,128)(2,1)}, u32[]{:S(2)}, u32[]{:S(2)}) async-start(bf16[128,2,1536]{2,1,0:T(2,128)(2,1)} %reshape.103), calls=%async_computation.1 | async-start | bytes 1572864 | tf_op jit(solution)/shard_map/all_to_all | solution.py:96
  49.9 505.6 %all-reduce.11.cloned.1.call-start = ((), (), s32[]{:S(2)}) async-start(), calls=%async_computation.4 | async-start | bytes 5308416 | tf_op jit(solution)/shard_map/psum | solution.py:157
  51.4 71.3 %copy-start.19 = (s32[256]{0:T(256)}, s32[256]{0:T(256)S(1)}, u32[]{:S(2)}) copy-start(s32[256]{0:T(256)S(1)} %eq.49) | copy-start | bytes 3076
  51.6 6.1 copy-start.17
  51.9 8.3 %copy-start.6 = (bf16[16,16,16,96]{3,2,1,0:T(8,128)(2,1)}, bf16[16,16,16,96]{3,2,1,0:T(8,128)(2,1)S(1)}, u32[]{:S(2)}) copy-start(bf16[16,16,16,96]{3,2,1,0:T(8,128)(2,1)S(1)} %fusion.59) | copy-start | bytes 2359300
  52.1 10.2 %collective-permute-start.8 = (bf16[1,16,1536]{2,1,0:T(8,128)(2,1)S(1)}, bf16[1,16,1536]{2,1,0:T(8,128)(2,1)S(1)}, u32[]{:S(2)}, u32[]{:S(2)}) collective-permute-start(bf16[1,16,1536]{2,1,0:T(8,128)(2,1)S(1)} %slice.931), channel_id=1, source_target_pairs={{0,16},{16,32},{32,48},{48,64},{64,80},{80,96},{96,112},{1,17},{17... | collective-permute-start | bytes 147464 | tf_op jit(solution)/shard_map/ppermute | solution.py:12
  60.4 5.8 collective-permute-start.9
  66.4 5.4 collective-permute-start.10
  69.4 5.5 collective-permute-start.11
  132.0 16.0 %collective-permute-start = (bf16[1,16,1536]{2,1,0:T(8,128)(2,1)}, bf16[1,16,1536]{2,1,0:T(8,128)(2,1)}, u32[]{:S(2)}, u32[]{:S(2)}) collective-permute-start(bf16[1,16,1536]{2,1,0:T(8,128)(2,1)} %slice.811), channel_id=1, source_target_pairs={{0,16},{16,32},{32,48},{48,64},{64,80},{80,96},{96,112},{1,17},{17... | collective-permute-start | bytes 147464 | tf_op jit(solution)/shard_map/ppermute | solution.py:12
  144.9 5.4 collective-permute-start.1
  150.5 13.4 %collective-permute-start.2 = (bf16[18,1,1536]{2,1,0:T(2,128)(2,1)S(1)}, bf16[18,1,1536]{2,1,0:T(2,128)(2,1)S(1)}, u32[]{:S(2)}, u32[]{:S(2)}) collective-permute-start(bf16[18,1,1536]{2,1,0:T(2,128)(2,1)S(1)} %get-tuple-element.24), channel_id=1, source_target_pairs={{0,1},{1,2},{2,3},{3,4},{4,5},{5,6},{6,7},{7,8},{8,9},{9,10},{10,1... | collective-permute-start | bytes 165896 | tf_op jit(solution)/shard_map/ppermute | solution.py:12
  153.9 10.0 %collective-permute-start.3 = (bf16[18,1,1536]{2,1,0:T(2,128)(2,1)S(1)}, bf16[18,1,1536]{2,1,0:T(2,128)(2,1)S(1)}, u32[]{:S(2)}, u32[]{:S(2)}) collective-permute-start(bf16[18,1,1536]{2,1,0:T(2,128)(2,1)S(1)} %get-tuple-element.25), channel_id=1, source_target_pairs={{1,0},{2,1},{3,2},{4,3},{5,4},{6,5},{7,6},{8,7},{9,8},{10,9},{11,1... | collective-permute-start | bytes 165896 | tf_op jit(solution)/shard_map/ppermute | solution.py:15
  259.4 43.0 %collective-permute-start.4 = (bf16[1,16,1536]{2,1,0:T(8,128)(2,1)S(1)}, bf16[1,16,1536]{2,1,0:T(8,128)(2,1)S(1)}, u32[]{:S(2)}, u32[]{:S(2)}) collective-permute-start(bf16[1,16,1536]{2,1,0:T(8,128)(2,1)S(1)} %slice.871), channel_id=1, source_target_pairs={{0,16},{16,32},{32,48},{48,64},{64,80},{80,96},{96,112},{1,17},{17... | collective-permute-start | bytes 147464 | tf_op jit(solution)/shard_map/ppermute | solution.py:12
  262.1 5.5 copy-start.4
  262.1 47.2 %collective-permute-start.12 = (bf16[1,16,1536]{2,1,0:T(8,128)(2,1)S(1)}, bf16[1,16,1536]{2,1,0:T(8,128)(2,1)S(1)}, u32[]{:S(2)}, u32[]{:S(2)}) collective-permute-start(bf16[1,16,1536]{2,1,0:T(8,128)(2,1)S(1)} %slice.991), channel_id=1, source_target_pairs={{0,16},{16,32},{32,48},{48,64},{64,80},{80,96},{96,112},{1,17},{17... | collective-permute-start | bytes 147464 | tf_op jit(solution)/shard_map/ppermute | solution.py:12
  298.4 5.4 collective-permute-start.5
  300.5 8.9 %collective-permute-start.13 = (bf16[1,16,1536]{2,1,0:T(8,128)(2,1)S(1)}, bf16[1,16,1536]{2,1,0:T(8,128)(2,1)S(1)}, u32[]{:S(2)}, u32[]{:S(2)}) collective-permute-start(bf16[1,16,1536]{2,1,0:T(8,128)(2,1)S(1)} %slice.993), channel_id=1, source_target_pairs={{16,0},{32,16},{48,32},{64,48},{80,64},{96,80},{112,96},{17,1},{33... | collective-permute-start | bytes 147464 | tf_op jit(solution)/shard_map/ppermute | solution.py:15
  304.0 11.8 %collective-permute-start.6 = (bf16[18,1,1536]{2,1,0:T(2,128)(2,1)S(1)}, bf16[18,1,1536]{2,1,0:T(2,128)(2,1)S(1)}, u32[]{:S(2)}, u32[]{:S(2)}) collective-permute-start(bf16[18,1,1536]{2,1,0:T(2,128)(2,1)S(1)} %get-tuple-element.22), channel_id=1, source_target_pairs={{0,1},{1,2},{2,3},{3,4},{4,5},{5,6},{6,7},{7,8},{8,9},{9,10},{10,1... | collective-permute-start | bytes 165896 | tf_op jit(solution)/shard_map/ppermute | solution.py:12
  308.0 7.8 %collective-permute-start.7 = (bf16[18,1,1536]{2,1,0:T(2,128)(2,1)S(1)}, bf16[18,1,1536]{2,1,0:T(2,128)(2,1)S(1)}, u32[]{:S(2)}, u32[]{:S(2)}) collective-permute-start(bf16[18,1,1536]{2,1,0:T(2,128)(2,1)S(1)} %get-tuple-element.23), channel_id=1, source_target_pairs={{1,0},{2,1},{3,2},{4,3},{5,4},{6,5},{7,6},{8,7},{9,8},{10,9},{11,1... | collective-permute-start | bytes 165896 | tf_op jit(solution)/shard_map/ppermute | solution.py:15
  309.4 6.4 copy-start.14
  309.6 51.1 %collective-permute-start.14 = (bf16[18,1,1536]{2,1,0:T(2,128)(2,1)S(1)}, bf16[18,1,1536]{2,1,0:T(2,128)(2,1)S(1)}, u32[]{:S(2)}, u32[]{:S(2)}) collective-permute-start(bf16[18,1,1536]{2,1,0:T(2,128)(2,1)S(1)} %get-tuple-element.18), channel_id=1, source_target_pairs={{0,1},{1,2},{2,3},{3,4},{4,5},{5,6},{6,7},{7,8},{8,9},{9,10},{10,1... | collective-permute-start | bytes 165896 | tf_op jit(solution)/shard_map/ppermute | solution.py:12
  314.5 46.2 %collective-permute-start.15 = (bf16[18,1,1536]{2,1,0:T(2,128)(2,1)S(1)}, bf16[18,1,1536]{2,1,0:T(2,128)(2,1)S(1)}, u32[]{:S(2)}, u32[]{:S(2)}) collective-permute-start(bf16[18,1,1536]{2,1,0:T(2,128)(2,1)S(1)} %get-tuple-element.19), channel_id=1, source_target_pairs={{1,0},{2,1},{3,2},{4,3},{5,4},{6,5},{7,6},{8,7},{9,8},{10,9},{11,1... | collective-permute-start | bytes 165896 | tf_op jit(solution)/shard_map/ppermute | solution.py:15
  481.2 111.9 %all-to-all-start.2 = ((bf16[128,2,1536]{2,1,0:T(2,128)(2,1)}), bf16[128,2,1536]{2,1,0:T(2,128)(2,1)S(1)}, u32[]{:S(2)}, u32[]{:S(2)}) async-start(bf16[128,2,1536]{2,1,0:T(2,128)(2,1)} %reshape.116), calls=%async_computation.2 | async-start | bytes 1572864 | tf_op jit(solution)/shard_map/all_to_all | solution.py:144
  494.4 159.1 %all-reduce.9.cloned.1.call-start = ((), (), s32[]{:S(2)}) async-start(), calls=%async_computation.3 | async-start | bytes 5308416 | tf_op jit(solution)/shard_map/psum | solution.py:157
  502.0 53.5 %copy-start.9 = (bf16[16,16,96,16]{2,3,1,0:T(8,128)(2,1)S(1)}, bf16[16,16,96,16]{2,3,1,0:T(8,128)(2,1)}, u32[]{:S(2)}) copy-start(bf16[16,16,96,16]{2,3,1,0:T(8,128)(2,1)} %copy.32) | copy-start | bytes 2359300
  581.4 12.1 %copy-start.22 = (s32[128]{0:T(128)S(1)}, s32[128]{0:T(128)}, u32[]{:S(2)}) copy-start(s32[128]{0:T(128)} %copy-done.21) | copy-start | bytes 1540
  (12 other events, 25.4 us)
Sparse Core Ops, SparseCore 0:
  479.1 76.3 all-reduce.10
  559.0 94.4 all-reduce.8
